TPU v7x, 32 devices: a whole 2x2x4 slice. The times are simulated.
32 devices in a mesh: lon: 16 (over z, x, core), lat: 2 (over y).
Axes of the slice: x: 2, y: 2, z: 4, core: 2. Of those that a mesh axis runs over, the one named last changes fastest.
Arguments:
- fields: bfloat16 [64, 1792, 256], P('lat', 'lon'), may hold values from -6 to 6
- cotangent: bfloat16 [64, 1792, 256], P('lat', 'lon'), may hold values from -6 to 6
- kernel: float32 [31, 256], replicated, may hold values from -1 to 1
- up_weight: bfloat16 [256, 1024], replicated, may hold values from -0.375 to 0.375
- down_weight: bfloat16 [1024, 256], replicated, may hold values from -0.1875 to 0.1875
Outputs:
- output: bfloat16 [64, 1792, 256], P('lat', 'lon')
- field_grad: bfloat16 [64, 1792, 256], P('lat', 'lon')
- kernel_grad: float32 [31, 256], replicated
- up_grad: float32 [256, 1024], replicated
- down_grad: float32 [1024, 256], replicated
All inputs are finite; a program needn't handle non-finite values.
Results may differ from a plain program's by a relative error of at most 0.0055.
Values may be sent and summed in bfloat16 or wider, within the bound.
No kernel may reach another device: no remote copies, remote signals or barrier semaphores. Data moves between devices by JAX's collectives and lax.ppermute only.
A program may use at most 128 MiB of HBM per device.

v0:
```python
import math
import jax
import jax.numpy as jnp
from jax import lax
from jax.sharding import PartitionSpec as P

KERNEL_SPACING = 4


def passed_along(value, axis, by):
    count = lax.axis_size(axis)
    return lax.ppermute(value, axis, [(i, (i + by) % count) for i in range(count)])


def gelu_tanh(values):
    return jax.nn.gelu(values, approximate=True)


def per_device(fields, cotangent, kernel, up_weight, down_weight):
    rows, column_list, channels = fields.shape
    taps = kernel.shape[0]
    taps_half_span = taps // 2
    border_extent = KERNEL_SPACING * taps_half_span
    blocks_out = -(-border_extent // column_list)
    sides = []
    for direction in (1, -1):
        current = fields
        current = passed_along(current, "lon", direction)
        passed = [current]
        sides.append(passed)
    whole = jnp.concatenate(sides[0][::-1] + [fields] + sides[1], axis=1)
    first = blocks_out * column_list - border_extent
    wrapped_input = whole[:, first : first + column_list + 2 * border_extent]
    conv = jnp.zeros((rows, column_list, channels), jnp.float32)
    for index_of_tap in range(taps):
        tap_window = wrapped_input[
            :, KERNEL_SPACING * index_of_tap : KERNEL_SPACING * index_of_tap + column_list
        ].astype(jnp.float32)
        conv = conv + kernel[index_of_tap] * tap_window
    conv = conv.reshape(rows * column_list, channels)
    center = jnp.mean(conv, axis=-1, keepdims=True)
    deviation = conv - center
    spread = jnp.mean(deviation * deviation, axis=-1, keepdims=True)
    inv_scale = lax.rsqrt(spread + 1e-06)
    normed = deviation * inv_scale
    normed_low = normed.astype(jnp.bfloat16)
    hidden = jnp.dot(normed_low, up_weight, preferred_element_type=jnp.float32)
    activated, pullback = jax.vjp(gelu_tanh, hidden)
    activated_low = activated.astype(jnp.bfloat16)
    flat_in = fields.reshape(rows * column_list, channels)
    flat_cot = cotangent.reshape(rows * column_list, channels)
    output = (
        flat_in.astype(jnp.float32)
        + jnp.dot(activated_low, down_weight, preferred_element_type=jnp.float32)
    ).astype(jnp.bfloat16)
    output = output.reshape(rows, column_list, channels)
    contract_last = (((1,), (1,)), ((), ()))
    contract_first = (((0,), (0,)), ((), ()))
    upstream = lax.dot_general(
        flat_cot, down_weight, contract_last, preferred_element_type=jnp.float32
    )
    hidden_grad = pullback(upstream)[0].astype(jnp.bfloat16)
    normed_grad = lax.dot_general(
        hidden_grad, up_weight, contract_last, preferred_element_type=jnp.float32
    )
    mean_grad = jnp.mean(normed_grad, axis=-1, keepdims=True)
    mean_cross = jnp.mean(normed_grad * normed, axis=-1, keepdims=True)
    conv_grad = (inv_scale * (normed_grad - mean_grad - normed * mean_cross)).reshape(
        rows, column_list, channels
    )
    layout = [(1, max(0, column_list - border_extent), column_list)]
    layout = layout + [(-1, 0, min(column_list, column_list + border_extent - column_list))]
    pieces = [
        passed_along(conv_grad[:, lower:upper].astype(jnp.bfloat16), "lon", moved).astype(
            jnp.float32
        )
        for moved, lower, upper in layout
    ]
    grad_padded = jnp.concatenate(pieces[:blocks_out] + [conv_grad] + pieces[blocks_out:], axis=1)
    conv_back = jnp.zeros((rows, column_list, channels), jnp.float32)
    for index_of_tap in range(taps):
        window_start = KERNEL_SPACING * (2 * taps_half_span - index_of_tap)
        conv_back = (
            conv_back
            + kernel[index_of_tap] * grad_padded[:, window_start : window_start + column_list]
        )
    field_grad = (cotangent.astype(jnp.float32) + conv_back).astype(jnp.bfloat16)
    kernel_terms = jnp.stack(
        [
            jnp.sum(
                wrapped_input[
                    :, KERNEL_SPACING * index_of_tap : KERNEL_SPACING * index_of_tap + column_list
                ].astype(jnp.float32)
                * conv_grad,
                axis=(0, 1),
            )
            for index_of_tap in range(taps)
        ]
    )
    grad_up = lax.dot_general(
        normed_low, hidden_grad, contract_first, preferred_element_type=jnp.float32
    )
    grad_down = lax.dot_general(
        activated_low, flat_cot, contract_first, preferred_element_type=jnp.float32
    )
    summed = lax.psum((kernel_terms, grad_up, grad_down), ("lon", "lat"))
    factor = 1.0 / math.sqrt(rows * column_list * lax.axis_size("lon") * lax.axis_size("lat"))
    return (output, field_grad, summed[0] * factor, summed[1] * factor, summed[2] * factor)


def solution(mesh):
    placed = (P("lat", "lon", None), P("lat", "lon", None), P(), P(), P())
    return jax.shard_map(
        per_device,
        mesh=mesh,
        in_specs=placed,
        out_specs=(P("lat", "lon", None), P("lat", "lon", None), P(), P(), P()),
        check_vma=False,
    )
```

profile of v0, /device:TPU:0, one launch (start us, length us, event | category | flops | bytes accessed | tf_op | source)
XLA Modules:
  0.0 282.3 jit_solution(12317122125374097740)
XLA Ops:
  7.2 0.0 copy-start
  7.2 0.0 copy-start.8
  7.2 0.0 all-reduce.3.cloned.1.call-start
  7.2 0.5 collective-permute-start
  7.7 5.0 %collective-permute-start.1 = (bf16[32,112,256]{2,1,0:T(8,128)(2,1)}, bf16[32,112,256]{2,1,0:T(8,128)(2,1)S(1)}, u32[]{:S(2)}, u32[]{:S(2)}) collective-permute-start(bf16[32,112,256]{2,1,0:T(8,128)(2,1)} %param.5), channel_id=1, source_target_pairs={{0,30},{2,0},{4,2},{6,4},{8,6},{10,8},{12,10},{14,12},{16,14},{18,... | collective-permute-start | bytes 5505032 | tf_op jit(solution)/shard_map/ppermute | solution.py:12
  12.8 1.0 fusion.165
  13.7 1.0 fusion.164
  14.8 19.2 %collective-permute-done = bf16[32,112,256]{2,1,0:T(8,128)(2,1)S(1)} collective-permute-done((bf16[32,112,256]{2,1,0:T(8,128)(2,1)}, bf16[32,112,256]{2,1,0:T(8,128)(2,1)S(1)}, u32[]{:S(2)}, u32[]{:S(2)}) %collective-permute-start) | collective-permute-done | bytes 1835040 | tf_op jit(solution)/shard_map/ppermute | solution.py:12
  33.9 0.2 constant_dynamic-update-slice_fusion.1
  34.2 0.3 constant_dynamic-update-slice_fusion
  34.5 0.0 collective-permute-done.1
  34.5 0.2 constant_dynamic-update-slice_fusion.2
  34.7 0.0 copy-start.1
  34.8 16.6 %fusion.161 = (f32[32,112]{1,0:T(8,128)S(1)}, f32[32,112,256]{2,1,0:T(8,128)}) fusion(bf16[32,224,256]{2,1,0:T(8,128)(2,1)S(1)} %constant_dynamic-update-slice_fusion.2, f32[256]{0:T(256)S(1)} %bitcast.116, f32[256]{0:T(256)S(1)} %bitcast.118, f32[256]{0:T(256)S(1)} %bitcast.122, f32[256]{0:T(256)S(1)} %bitcast.124, f32[256]{0:T(256)S(1)} %bitcast.126, ...), kind=kLoop, calls=%fused_computation.300 | loop fusion | flops 85324288 | bytes 60601344 | tf_op jit(solution)/shard_map/reduce_sum | solution.py:41
  51.3 0.0 copy-done.1
  51.4 0.1 div.15
  51.4 2.7 multiply_reduce_fusion.2
  54.2 0.1 rsqrt.12
  54.3 3.4 %fusion.159 = bf16[3584,256]{1,0:T(8,128)(2,1)S(1)} fusion(f32[32,112,256]{2,1,0:T(8,128)} %get-tuple-element.41, f32[3584]{0:T(1024)S(1)} %rsqrt.12, f32[3584]{0:T(1024)S(1)} %div.15), kind=kLoop, calls=%fused_computation.287 | loop fusion | flops 2752512 | bytes 5533696 | tf_op jit(solution)/shard_map/convert_element_type | solution.py:46
  57.7 0.0 copy-done
  57.7 0.0 copy-start.11
  57.7 7.9 %multiply_convert_fusion = (bf16[3584,1024]{1,0:T(8,128)(2,1)S(1)}, f32[3584,1024]{1,0:T(8,128)}) fusion(bf16[3584,256]{1,0:T(8,128)(2,1)S(1)} %fusion.159, bf16[256,1024]{1,0:T(8,128)(2,1)S(1)} %copy-done), kind=kOutput, calls=%fused_computation.65 | convolution fusion | flops 1912078336 | bytes 24379392 | tf_op jit(solution)/shard_map/dot_general | solution.py:47
  65.6 15.9 %fusion.6 = bf16[3584,1024]{1,0:T(8,128)(2,1)S(1)} fusion(f32[3584,1024]{1,0:T(8,128)} %get-tuple-element.78, bf16[3584,256]{1,0:T(8,128)(2,1)} %bitcast.94, bf16[1024,256]{1,0:T(8,128)(2,1)S(1)} %copy-done.11), kind=kOutput, calls=%fused_computation.64 | convolution fusion | flops 1952448512 | bytes 24379392 | tf_op jit(solution)/shard_map/dot_general | solution.py:59
  81.5 0.0 copy-done.7
  81.5 2.5 fusion.160
  84.0 2.7 subtract_multiply_fusion
  86.7 9.4 %fusion.47 = (f32[256]{0:T(256)}, f32[256]{0:T(256)}, f32[256]{0:T(256)}, f32[256]{0:T(256)}, f32[256]{0:T(256)}, /*index=5*/f32[256]{0:T(256)}, f32[256]{0:T(25...) fusion(f32[32,112,256]{2,1,0:T(8,128)S(1)} %bitcast.89, ...), kind=kLoop, calls=%fused_computation.167 | loop fusion | flops 41283840 | bytes 31210496 | tf_op jit(solution)/shard_map/reduce_sum | solution.py:90
  96.1 0.0 copy-done.2
  96.1 9.5 %fusion.67 = (f32[256]{0:T(256)S(1)}, f32[256]{0:T(256)S(1)}, f32[256]{0:T(256)S(1)}, f32[256]{0:T(256)S(1)}, f32[256]{0:T(256)S(1)}, /*index=5*/f32[256]{0:T(25...) fusion(f32[32,112,256]{2,1,0:T(8,128)S(1)} %bitcast.90, ...), kind=kLoop, calls=%fused_computation.187 | loop fusion | flops 44036096 | bytes 33046528 | tf_op jit(solution)/shard_map/reduce_sum | solution.py:90
  105.7 2.0 copy.14
  107.6 3.1 %fusion.167 = f32[1024,256]{1,0:T(8,128)} fusion(bf16[3584,1024]{1,0:T(8,128)(2,1)S(1)} %get-tuple-element.77, bf16[3584,256]{1,0:T(8,128)(2,1)S(1)} %bitcast.95), kind=kOutput, calls=%fused_computation.305 | convolution fusion | flops 1879048192 | bytes 10223616 | tf_op jit(solution)/shard_map/dot_general | solution.py:103
  110.7 1.5 fusion.163
  112.2 3.9 %collective-permute-start.2 = (bf16[32,60,256]{2,0,1:T(8,128)(2,1)}, bf16[32,60,256]{2,0,1:T(8,128)(2,1)S(1)}, u32[]{:S(2)}, u32[]{:S(2)}) collective-permute-start(bf16[32,60,256]{2,0,1:T(8,128)(2,1)} %get-tuple-element.42), channel_id=1, source_target_pairs={{0,30},{2,0},{4,2},{6,4},{8,6},{10,8},{12,10},{14,12},{16,14},{18,... | collective-permute-start | bytes 2949128 | tf_op jit(solution)/shard_map/ppermute | solution.py:12
  116.1 14.4 %collective-permute-start.3 = (bf16[32,60,256]{2,0,1:T(8,128)(2,1)}, bf16[32,60,256]{2,0,1:T(8,128)(2,1)}, u32[]{:S(2)}, u32[]{:S(2)}) collective-permute-start(bf16[32,60,256]{2,0,1:T(8,128)(2,1)} %get-tuple-element.43), channel_id=1, source_target_pairs={{0,2},{2,4},{4,6},{6,8},{8,10},{10,12},{12,14},{14,16},{16,18},{18... | collective-permute-start | bytes 2949128 | tf_op jit(solution)/shard_map/ppermute | solution.py:12
  130.6 3.0 %fusion.166 = f32[256,1024]{1,0:T(8,128)} fusion(bf16[3584,256]{1,0:T(8,128)(2,1)S(1)} %fusion.159, bf16[3584,1024]{1,0:T(8,128)(2,1)S(1)} %fusion.6), kind=kOutput, calls=%fused_computation.304 | convolution fusion | flops 1879048192 | bytes 10223616 | tf_op jit(solution)/shard_map/dot_general | solution.py:100
  133.6 0.0 all-reduce.3.cloned.1.call-update
  133.6 2.8 %stack.127 = f32[31,256]{1,0:T(8,128)S(1)} concatenate(f32[1,256]{1,0:T(1,128)} %bitcast.188, f32[1,256]{1,0:T(1,128)} %bitcast.187, f32[1,256]{1,0:T(1,128)} %bitcast.186, f32[1,256]{1,0:T(1,128)} %bitcast.185, f32[1,256]{1,0:T(1,128)} %bitcast.184, f32[1,256]{1,0:T(1,128)} %bitcast.183, f32[1,256]{1,0:T(1,128)} %bitcast.182, f32[1,256]{1,0:T(1,128)} %bitcast.181, ...), dimensions={0} | concatenate | bytes 63488 | tf_op jit(solution)/shard_map/stack | solution.py:88
  136.5 56.0 %psum.21 = f32[31,256]{1,0:T(8,128)S(1)} all-reduce(f32[31,256]{1,0:T(8,128)S(1)} %stack.127), channel_id=1, replica_groups=mesh['lon'=16,'lat'=2] {'lon','lat'}, use_global_device_ids=true, to_apply=%region_35.0 | all-reduce | flops 7936 | bytes 63488 | tf_op jit(solution)/shard_map/psum | solution.py:106
  192.5 0.6 broadcast_multiply_fusion.2
  193.1 6.5 %fusion.7 = bf16[3584,256]{1,0:T(8,128)(2,1)} fusion(bf16[3584,1024]{1,0:T(8,128)(2,1)} %copy-done.9, bf16[1024,256]{1,0:T(8,128)(2,1)} %param.9, bf16[3584,256]{1,0:T(8,128)(2,1)S(1)} %bitcast.93), kind=kOutput, calls=%fused_computation.67 | convolution fusion | flops 1881800704 | bytes 11534336 | tf_op jit(solution)/shard_map/dot_general | solution.py:54
  199.6 0.0 collective-permute-done.3
  199.6 1.9 copy.12
  201.5 0.0 collective-permute-done.2
  201.5 0.6 copy.11
  202.1 22.8 %fusion.73 = bf16[32,112,256]{2,1,0:T(8,128)(2,1)} fusion(f32[32,112,256]{2,1,0:T(8,128)S(1)} %bitcast.92, f32[32,60,256]{2,1,0:T(8,128)S(1)} %copy.12, f32[32,60,256]{2,1,0:T(8,128)S(1)} %copy.11, bf16[32,112,256]{2,1,0:T(8,128)(2,1)} %param.6, f32[256]{0:T(256)S(1)} %bitcast.117, f32[256]{0:T(256)S(1)} %bitcast.119, f32[256]{0:T(256)S(1)} %bitcast.123, ...), kind=kLoop, calls=%fused_computation.193 | loop fusion | flops 86245376 | bytes 11303936 | tf_op jit(solution)/shard_map/convert_element_type | solution.py:87
  224.9 45.9 %all-reduce.3.cloned.1.call-done = (f32[256,1024]{1,0:T(8,128)}, f32[1024,256]{1,0:T(8,128)}) async-done(((f32[256,1024]{1,0:T(8,128)}, f32[1024,256]{1,0:T(8,128)}), (f32[256,1024]{1,0:T(8,128)}, f32[1024,256]{1,0:T(8,128)})) %all-reduce.3.cloned.1.call-update) | async-done | bytes 2097168 | tf_op jit(solution)/shard_map/psum | solution.py:106
  270.8 2.3 broadcast_multiply_fusion.1
  273.2 2.3 broadcast_multiply_fusion
  (19 shorter events, 0.1 us)
Async XLA Ops:
  7.2 50.5 %copy-start = (bf16[256,1024]{1,0:T(8,128)(2,1)S(1)}, bf16[256,1024]{1,0:T(8,128)(2,1)}, u32[]{:S(2)}) copy-start(bf16[256,1024]{1,0:T(8,128)(2,1)} %param.8) | copy-start | bytes 1572868
  7.2 27.0 %copy-start.8 = (bf16[32,112,256]{2,1,0:T(8,128)(2,1)S(1)}, bf16[32,112,256]{2,1,0:T(8,128)(2,1)}, u32[]{:S(2)}) copy-start(bf16[32,112,256]{2,1,0:T(8,128)(2,1)} %param.5) | copy-start | bytes 5505028
  7.2 263.6 %all-reduce.3.cloned.1.call-start = ((), (), s32[]{:S(2)}) async-start(), calls=%async_computation | async-start | bytes 4194304 | tf_op jit(solution)/shard_map/psum | solution.py:106
  7.2 26.7 %collective-permute-start = (bf16[32,112,256]{2,1,0:T(8,128)(2,1)}, bf16[32,112,256]{2,1,0:T(8,128)(2,1)S(1)}, u32[]{:S(2)}, u32[]{:S(2)}) collective-permute-start(bf16[32,112,256]{2,1,0:T(8,128)(2,1)} %param.5), channel_id=1, source_target_pairs={{0,2},{2,4},{4,6},{6,8},{8,10},{10,12},{12,14},{14,16},{16,18},{18... | collective-permute-start | bytes 5505032 | tf_op jit(solution)/shard_map/ppermute | solution.py:12
  7.7 26.8 %collective-permute-start.1 = (bf16[32,112,256]{2,1,0:T(8,128)(2,1)}, bf16[32,112,256]{2,1,0:T(8,128)(2,1)S(1)}, u32[]{:S(2)}, u32[]{:S(2)}) collective-permute-start(bf16[32,112,256]{2,1,0:T(8,128)(2,1)} %param.5), channel_id=1, source_target_pairs={{0,30},{2,0},{4,2},{6,4},{8,6},{10,8},{12,10},{14,12},{16,14},{18,... | collective-permute-start | bytes 5505032 | tf_op jit(solution)/shard_map/ppermute | solution.py:12
  34.5 16.9 %copy-start.3 = (bf16[32,224,256]{2,1,0:T(8,128)(2,1)}, bf16[32,224,256]{2,1,0:T(8,128)(2,1)S(1)}, u32[]{:S(2)}) copy-start(bf16[32,224,256]{2,1,0:T(8,128)(2,1)S(1)} %get-tuple-element.44) | copy-start | bytes 11010052
  34.7 16.6 %copy-start.1 = (bf16[32,224,256]{2,1,0:T(8,128)(2,1)}, bf16[32,224,256]{2,1,0:T(8,128)(2,1)S(1)}, u32[]{:S(2)}) copy-start(bf16[32,224,256]{2,1,0:T(8,128)(2,1)S(1)} %constant_dynamic-update-slice_fusion.2) | copy-start | bytes 11010052
  57.7 7.9 %copy-start.11 = (bf16[1024,256]{1,0:T(8,128)(2,1)S(1)}, bf16[1024,256]{1,0:T(8,128)(2,1)}, u32[]{:S(2)}) copy-start(bf16[1024,256]{1,0:T(8,128)(2,1)} %param.9) | copy-start | bytes 1572868
  65.6 42.0 %copy-start.9 = (bf16[3584,1024]{1,0:T(8,128)(2,1)}, bf16[3584,1024]{1,0:T(8,128)(2,1)S(1)}, u32[]{:S(2)}) copy-start(bf16[3584,1024]{1,0:T(8,128)(2,1)S(1)} %get-tuple-element.77) | copy-start | bytes 22020100
  65.6 15.9 %copy-start.7 = (f32[32,112,256]{2,1,0:T(8,128)S(1)}, f32[32,112,256]{2,1,0:T(8,128)}, u32[]{:S(2)}) copy-start(f32[32,112,256]{2,1,0:T(8,128)} %get-tuple-element.41) | copy-start | bytes 11010052
  84.0 2.7 copy-start.4
  86.7 19.0 %copy-start.5 = (f32[3584,256]{1,0:T(8,128)}, f32[3584,256]{1,0:T(8,128)S(1)}, u32[]{:S(2)}) copy-start(f32[3584,256]{1,0:T(8,128)S(1)} %subtract_multiply_fusion) | copy-start | bytes 11010052
  86.7 9.4 %copy-start.2 = (bf16[32,224,256]{2,1,0:T(8,128)(2,1)S(1)}, bf16[32,224,256]{2,1,0:T(8,128)(2,1)}, u32[]{:S(2)}) copy-start(bf16[32,224,256]{2,1,0:T(8,128)(2,1)} %copy-done.1) | copy-start | bytes 11010052
  105.7 2.0 copy-start.10
  112.2 89.3 %collective-permute-start.2 = (bf16[32,60,256]{2,0,1:T(8,128)(2,1)}, bf16[32,60,256]{2,0,1:T(8,128)(2,1)S(1)}, u32[]{:S(2)}, u32[]{:S(2)}) collective-permute-start(bf16[32,60,256]{2,0,1:T(8,128)(2,1)} %get-tuple-element.42), channel_id=1, source_target_pairs={{0,30},{2,0},{4,2},{6,4},{8,6},{10,8},{12,10},{14,12},{16,14},{18,... | collective-permute-start | bytes 2949128 | tf_op jit(solution)/shard_map/ppermute | solution.py:12
  116.1 83.5 %collective-permute-start.3 = (bf16[32,60,256]{2,0,1:T(8,128)(2,1)}, bf16[32,60,256]{2,0,1:T(8,128)(2,1)}, u32[]{:S(2)}, u32[]{:S(2)}) collective-permute-start(bf16[32,60,256]{2,0,1:T(8,128)(2,1)} %get-tuple-element.43), channel_id=1, source_target_pairs={{0,2},{2,4},{4,6},{6,8},{8,10},{10,12},{12,14},{14,16},{16,18},{18... | collective-permute-start | bytes 2949128 | tf_op jit(solution)/shard_map/ppermute | solution.py:12
  199.6 2.5 copy-start.6
Sparse Core Ops, SparseCore 0:
  133.7 137.0 all-reduce.2
where the time goes:
time: 283 us; the launch traced here: 282 us
  other arithmetic  72.4 us (26%)
  waiting for transfers between devices  65.1 us (23%)
  blocking collectives  56 us (20%)
  matrix products  38.9 us (14%)
  starting transfers between devices  23.9 us (8%)
  between operations  14.3 us (5%)
  local copies, waits for them, and re-layouts  11.7 us (4%)
    psum x1, blocking collectives, per_device(): summed = lax.psum((kernel_terms, grad_up, grad_down), ('lon', 'lat'))  56 us
    psum x1, waiting for transfers between devices, per_device(): summed = lax.psum((kernel_terms, grad_up, grad_down), ('lon', 'lat'))  45.9 us
    ppermute x4, starting transfers between devices, passed_along(): lax.ppermute(value, axis, [(i, (i + by) % count) for i in range(count)])  23.9 us
    convert_element_type x1, other arithmetic, per_device(): (cotangent.astype(jnp.float32) + conv_back).astype(jnp.bfloat16)  22.8 us
    ppermute x4, waiting for transfers between devices, passed_along(): lax.ppermute(value, axis, [(i, (i + by) % count) for i in range(count)])  19.2 us
    reduce_sum x2, other arithmetic, per_device(): jnp.sum(wrapped_input[:, KERNEL_SPACING * index_of_tap:KERNEL_SPACING * i...  18.9 us
    reduce_sum x1, other arithmetic, per_device(): center = jnp.mean(conv, axis=-1, keepdims=True)  16.6 us
    dot_general x1, matrix products, per_device(): lax.dot_general(flat_cot, down_weight, contract_last, preferred_element_t...  15.9 us
  transfers between devices with their start and end apart: 5, of which 2 were waited for; matrix products, arithmetic and copies ran while one was open for 14% of the time, Pallas kernels for 0%

commit v1 on v0

--- a/solution.py
+++ b/solution.py
@@ -103,7 +103,7 @@
     grad_down = lax.dot_general(
         activated_low, flat_cot, contract_first, preferred_element_type=jnp.float32
     )
-    summed = lax.psum((kernel_terms, grad_up, grad_down), ("lon", "lat"))
+    summed = lax.psum(lax.psum((kernel_terms, grad_up, grad_down), "lat"), "lon")
     factor = 1.0 / math.sqrt(rows * column_list * lax.axis_size("lon") * lax.axis_size("lat"))
     return (output, field_grad, summed[0] * factor, summed[1] * factor, summed[2] * factor)
 

time: 283 us -> 341 us (1.20)
  other arithmetic: 72.4 us -> 109 us
  blocking collectives: 56 us -> 68.9 us
  local copies, waits for them, and re-layouts: 11.7 us -> 16.5 us
    convert_element_type x1, other arithmetic: 22.8 us -> 47 us  [per_device(): (cotangent.astype(jnp.float32) + conv_back).astype(jnp.bfloat16)]
    psum x1 -> x2, blocking collectives: 56 us -> 68.9 us  [the longest x1 59.8 us: per_device(): lax.psum(lax.psum((kernel_terms, grad_up, grad_down), 'lat'), 'lon')]
    reduce_sum x2, other arithmetic: 18.9 us -> 28.4 us  [per_device(): jnp.sum(wrapped_input[:, KERNEL_SPACING * index_of_tap:KERNEL_SPACING * i...]
    psum x1 -> x2, waiting for transfers between devices: 45.9 us -> 47.3 us  [the longest x1 47.3 us: per_device(): lax.psum(lax.psum((kernel_terms, grad_up, grad_down), 'lat'), 'lon')]
  transfers between devices with their start and end apart: 5 -> 6, of which waited for: 2 -> 2; matrix products, arithmetic and copies ran while one was open for 14% -> 24% of each run, Pallas kernels for 0% -> 0%
where the time goes in v1:
time: 341 us; the launch traced here: 340 us
  other arithmetic  109 us (32%)
  blocking collectives  68.9 us (20%)
  waiting for transfers between devices  66.5 us (20%)
  matrix products  41.2 us (12%)
  starting transfers between devices  24 us (7%)
  local copies, waits for them, and re-layouts  16.5 us (5%)
  between operations  14.2 us (4%)
    psum x1, blocking collectives, per_device(): lax.psum(lax.psum((kernel_terms, grad_up, grad_down), 'lat'), 'lon')  59.8 us
    psum x1, waiting for transfers between devices, per_device(): lax.psum(lax.psum((kernel_terms, grad_up, grad_down), 'lat'), 'lon')  47.3 us
    convert_element_type x1, other arithmetic, per_device(): (cotangent.astype(jnp.float32) + conv_back).astype(jnp.bfloat16)  47 us
    reduce_sum x2, other arithmetic, per_device(): jnp.sum(wrapped_input[:, KERNEL_SPACING * index_of_tap:KERNEL_SPACING * i...  28.4 us
    ppermute x4, starting transfers between devices, passed_along(): lax.ppermute(value, axis, [(i, (i + by) % count) for i in range(count)])  23.9 us
    ppermute x4, waiting for transfers between devices, passed_along(): lax.ppermute(value, axis, [(i, (i + by) % count) for i in range(count)])  19.2 us
    reduce_sum x1, other arithmetic, per_device(): center = jnp.mean(conv, axis=-1, keepdims=True)  16.6 us
    dot_general x1, matrix products, per_device(): lax.dot_general(flat_cot, down_weight, contract_last, preferred_element_t...  15.3 us
  transfers between devices with their start and end apart: 6, of which 2 were waited for; matrix products, arithmetic and copies ran while one was open for 24% of the time, Pallas kernels for 0%

profile of v1, /device:TPU:0, one launch (start us, length us, event | category | flops | bytes accessed | tf_op | source)
XLA Modules:
  0.0 340.2 jit_solution(14359421557109993822)
XLA Ops:
  7.2 0.0 copy-start
  7.2 0.0 all-reduce.7.cloned.1.call-start
  7.2 0.5 collective-permute-start
  7.7 5.0 %collective-permute-start.1 = (bf16[32,112,256]{2,1,0:T(8,128)(2,1)}, bf16[32,112,256]{2,1,0:T(8,128)(2,1)S(1)}, u32[]{:S(2)}, u32[]{:S(2)}) collective-permute-start(bf16[32,112,256]{2,1,0:T(8,128)(2,1)} %param.5), channel_id=1, source_target_pairs={{0,30},{2,0},{4,2},{6,4},{8,6},{10,8},{12,10},{14,12},{16,14},{18,... | collective-permute-start | bytes 5505032 | tf_op jit(solution)/shard_map/ppermute | solution.py:12
  12.8 1.0 fusion.165
  13.7 1.0 fusion.164
  14.8 19.2 %collective-permute-done = bf16[32,112,256]{2,1,0:T(8,128)(2,1)S(1)} collective-permute-done((bf16[32,112,256]{2,1,0:T(8,128)(2,1)}, bf16[32,112,256]{2,1,0:T(8,128)(2,1)S(1)}, u32[]{:S(2)}, u32[]{:S(2)}) %collective-permute-start) | collective-permute-done | bytes 1835040 | tf_op jit(solution)/shard_map/ppermute | solution.py:12
  33.9 0.2 constant_dynamic-update-slice_fusion.1
  34.2 0.3 constant_dynamic-update-slice_fusion
  34.5 0.0 collective-permute-done.1
  34.5 0.2 constant_dynamic-update-slice_fusion.2
  34.7 0.0 copy-start.1
  34.8 16.6 %fusion.161 = (f32[32,112]{1,0:T(8,128)S(1)}, f32[32,112,256]{2,1,0:T(8,128)}) fusion(bf16[32,224,256]{2,1,0:T(8,128)(2,1)S(1)} %constant_dynamic-update-slice_fusion.2, f32[256]{0:T(256)S(1)} %bitcast.116, f32[256]{0:T(256)S(1)} %bitcast.118, f32[256]{0:T(256)S(1)} %bitcast.122, f32[256]{0:T(256)S(1)} %bitcast.124, f32[256]{0:T(256)S(1)} %bitcast.126, ...), kind=kLoop, calls=%fused_computation.300 | loop fusion | flops 85324288 | bytes 60601344 | tf_op jit(solution)/shard_map/reduce_sum | solution.py:41
  51.3 0.0 copy-done.1
  51.4 0.1 div.15
  51.4 2.7 multiply_reduce_fusion.2
  54.2 0.1 rsqrt.12
  54.3 3.4 %fusion.159 = bf16[3584,256]{1,0:T(8,128)(2,1)S(1)} fusion(f32[32,112,256]{2,1,0:T(8,128)} %get-tuple-element.43, f32[3584]{0:T(1024)S(1)} %rsqrt.12, f32[3584]{0:T(1024)S(1)} %div.15), kind=kLoop, calls=%fused_computation.287 | loop fusion | flops 2752512 | bytes 5533696 | tf_op jit(solution)/shard_map/convert_element_type | solution.py:46
  57.7 0.0 copy-start.8
  57.7 0.0 copy-start.9
  57.7 7.9 %multiply_convert_fusion = (bf16[3584,1024]{1,0:T(8,128)(2,1)S(1)}, f32[3584,1024]{1,0:T(8,128)}) fusion(bf16[3584,256]{1,0:T(8,128)(2,1)S(1)} %fusion.159, bf16[256,1024]{1,0:T(8,128)(2,1)S(1)} %copy-done), kind=kOutput, calls=%fused_computation.65 | convolution fusion | flops 1912078336 | bytes 24379392 | tf_op jit(solution)/shard_map/dot_general | solution.py:47
  65.6 15.3 %fusion.6 = bf16[3584,1024]{1,0:T(8,128)(2,1)S(1)} fusion(f32[3584,1024]{1,0:T(8,128)} %get-tuple-element.80, bf16[3584,256]{1,0:T(8,128)(2,1)S(1)} %bitcast.94, bf16[1024,256]{1,0:T(8,128)(2,1)S(1)} %copy-done.9), kind=kOutput, calls=%fused_computation.64 | convolution fusion | flops 1952448512 | bytes 24379392 | tf_op jit(solution)/shard_map/dot_general | solution.py:59
  81.0 3.0 fusion.166
  84.0 5.5 %fusion.160 = (f32[3584]{0:T(1024)S(1)}, f32[3584]{0:T(1024)S(1)}, f32[3584,256]{1,0:T(8,128)}) fusion(f32[3584]{0:T(1024)S(1)} %rsqrt.12, f32[3584]{0:T(1024)S(1)} %div.15, f32[32,112,256]{2,1,0:T(8,128)S(1)} %copy-done.5, bf16[3584,1024]{1,0:T(8,128)(2,1)S(1)} %fusion.6, bf16[256,1024]{1,0:T(8,128)(2,1)S(1)} %copy-done), kind=kOutput, calls=%fused_computation.299 | convolution fusion | flops 1883628544 | bytes 15261696 | tf_op jit(solution)/shard_map/dot_general | solution.py:63
  89.5 5.4 %subtract_multiply_fusion = f32[3584,256]{1,0:T(8,128)S(1)} fusion(f32[3584,256]{1,0:T(8,128)} %get-tuple-element.81, f32[32,112,256]{2,1,0:T(8,128)S(1)} %copy-done.5, f32[3584]{0:T(1024)S(1)} %get-tuple-element.82, f32[3584]{0:T(1024)S(1)} %get-tuple-element.83, f32[3584]{0:T(1024)S(1)} %rsqrt.12, f32[3584]{0:T(1024)S(1)} %div.15), kind=kLoop, calls=%fused_computation.284 | loop fusion | flops 5505024 | bytes 11067392 | tf_op jit(solution)/shard_map/mul | solution.py:68
  94.9 9.6 %fusion.67 = (f32[256]{0:T(256)S(1)}, f32[256]{0:T(256)S(1)}, f32[256]{0:T(256)S(1)}, f32[256]{0:T(256)S(1)}, f32[256]{0:T(256)S(1)}, /*index=5*/f32[256]{0:T(25...) fusion(f32[32,112,256]{2,1,0:T(8,128)S(1)} %bitcast.89, ...), kind=kLoop, calls=%fused_computation.187 | loop fusion | flops 44036096 | bytes 33046528 | tf_op jit(solution)/shard_map/reduce_sum | solution.py:90
  104.4 3.2 copy.14
  107.6 3.1 fusion.167
  110.7 2.6 fusion.163
  113.3 3.9 %collective-permute-start.2 = (bf16[32,60,256]{2,0,1:T(8,128)(2,1)}, bf16[32,60,256]{2,0,1:T(8,128)(2,1)}, u32[]{:S(2)}, u32[]{:S(2)}) collective-permute-start(bf16[32,60,256]{2,0,1:T(8,128)(2,1)} %get-tuple-element.44), channel_id=1, source_target_pairs={{0,30},{2,0},{4,2},{6,4},{8,6},{10,8},{12,10},{14,12},{16,14},{18,... | collective-permute-start | bytes 2949128 | tf_op jit(solution)/shard_map/ppermute | solution.py:12
  117.2 14.4 %collective-permute-start.3 = (bf16[32,60,256]{2,0,1:T(8,128)(2,1)S(1)}, bf16[32,60,256]{2,0,1:T(8,128)(2,1)}, u32[]{:S(2)}, u32[]{:S(2)}) collective-permute-start(bf16[32,60,256]{2,0,1:T(8,128)(2,1)S(1)} %get-tuple-element.45), channel_id=1, source_target_pairs={{0,2},{2,4},{4,6},{6,8},{8,10},{10,12},{12,14},{14,16},{16,18},{18... | collective-permute-start | bytes 2949128 | tf_op jit(solution)/shard_map/ppermute | solution.py:12
  131.6 0.0 all-reduce.7.cloned.1.call-update
  131.7 0.0 all-reduce.5.cloned.1.call-start
  131.7 18.9 %fusion.47 = (f32[256]{0:T(256)}, f32[256]{0:T(256)}, f32[256]{0:T(256)}, f32[256]{0:T(256)}, f32[256]{0:T(256)}, /*index=5*/f32[256]{0:T(256)}, f32[256]{0:T(25...) fusion(f32[32,112,256]{2,1,0:T(8,128)} %bitcast.91, ...), kind=kLoop, calls=%fused_computation.167 | loop fusion | flops 41283840 | bytes 31210496 | tf_op jit(solution)/shard_map/reduce_sum | solution.py:90
  150.6 2.9 stack.127
  153.5 9.1 %psum.42 = f32[31,256]{1,0:T(8,128)S(1)} all-reduce(f32[31,256]{1,0:T(8,128)S(1)} %stack.127), channel_id=1, replica_groups=mesh['lon'=16,'lat'=2] {'lat'}, use_global_device_ids=true, to_apply=%region_35.0 | all-reduce | flops 7936 | bytes 63488 | tf_op jit(solution)/shard_map/psum | solution.py:106
  162.6 59.8 %psum.43 = f32[31,256]{1,0:T(8,128)S(1)} all-reduce(f32[31,256]{1,0:T(8,128)S(1)} %psum.42), channel_id=1, replica_groups=mesh['lon'=16,'lat'=2] {'lon'}, use_global_device_ids=true, to_apply=%region_36.0 | all-reduce | flops 7936 | bytes 63488 | tf_op jit(solution)/shard_map/psum | solution.py:106
  222.4 0.6 broadcast_multiply_fusion.2
  223.0 6.4 %fusion.7 = bf16[3584,256]{1,0:T(8,128)(2,1)} fusion(bf16[3584,1024]{1,0:T(8,128)(2,1)} %copy-done.7, bf16[1024,256]{1,0:T(8,128)(2,1)} %param.9, bf16[3584,256]{1,0:T(8,128)(2,1)S(1)} %bitcast.93), kind=kOutput, calls=%fused_computation.67 | convolution fusion | flops 1881800704 | bytes 11534336 | tf_op jit(solution)/shard_map/dot_general | solution.py:54
  229.5 0.0 collective-permute-done.3
  229.5 1.8 copy.12
  231.2 0.0 collective-permute-done.2
  231.2 3.1 copy.11
  234.4 0.0 all-reduce.5.cloned.1.call-update
  234.4 47.0 %fusion.73 = bf16[32,112,256]{2,1,0:T(8,128)(2,1)} fusion(f32[32,112,256]{2,1,0:T(8,128)} %bitcast.92, f32[32,60,256]{2,1,0:T(8,128)S(1)} %copy.12, f32[32,60,256]{2,1,0:T(8,128)} %copy.11, bf16[32,112,256]{2,1,0:T(8,128)(2,1)} %param.6, f32[256]{0:T(256)S(1)} %bitcast.117, f32[256]{0:T(256)S(1)} %bitcast.119, f32[256]{0:T(256)S(1)} %bitcast.123, ...), kind=kLoop, calls=%fused_computation.193 | loop fusion | flops 86245376 | bytes 11303936 | tf_op jit(solution)/shard_map/convert_element_type | solution.py:87
  281.4 47.3 %all-reduce.5.cloned.1.call-done = (f32[256,1024]{1,0:T(8,128)}, f32[1024,256]{1,0:T(8,128)}) async-done(((f32[256,1024]{1,0:T(8,128)}, f32[1024,256]{1,0:T(8,128)}), (f32[256,1024]{1,0:T(8,128)}, f32[1024,256]{1,0:T(8,128)})) %all-reduce.5.cloned.1.call-update) | async-done | bytes 2097168 | tf_op jit(solution)/shard_map/psum | solution.py:106
  328.7 2.3 broadcast_multiply_fusion.1
  331.0 2.3 broadcast_multiply_fusion
  (19 shorter events, 0.0 us)
Async XLA Ops:
  7.2 50.5 %copy-start = (bf16[256,1024]{1,0:T(8,128)(2,1)S(1)}, bf16[256,1024]{1,0:T(8,128)(2,1)}, u32[]{:S(2)}) copy-start(bf16[256,1024]{1,0:T(8,128)(2,1)} %param.8) | copy-start | bytes 1572868
  7.2 27.0 %copy-start.6 = (bf16[32,112,256]{2,1,0:T(8,128)(2,1)S(1)}, bf16[32,112,256]{2,1,0:T(8,128)(2,1)}, u32[]{:S(2)}) copy-start(bf16[32,112,256]{2,1,0:T(8,128)(2,1)} %param.5) | copy-start | bytes 5505028
  7.2 227.2 %all-reduce.7.cloned.1.call-start = ((), (), s32[]{:S(2)}) async-start(), calls=%async_computation.1 | async-start | bytes 4194304 | tf_op jit(solution)/shard_map/psum | solution.py:106
  7.2 26.7 %collective-permute-start = (bf16[32,112,256]{2,1,0:T(8,128)(2,1)}, bf16[32,112,256]{2,1,0:T(8,128)(2,1)S(1)}, u32[]{:S(2)}, u32[]{:S(2)}) collective-permute-start(bf16[32,112,256]{2,1,0:T(8,128)(2,1)} %param.5), channel_id=1, source_target_pairs={{0,2},{2,4},{4,6},{6,8},{8,10},{10,12},{12,14},{14,16},{16,18},{18... | collective-permute-start | bytes 5505032 | tf_op jit(solution)/shard_map/ppermute | solution.py:12
  7.7 26.8 %collective-permute-start.1 = (bf16[32,112,256]{2,1,0:T(8,128)(2,1)}, bf16[32,112,256]{2,1,0:T(8,128)(2,1)S(1)}, u32[]{:S(2)}, u32[]{:S(2)}) collective-permute-start(bf16[32,112,256]{2,1,0:T(8,128)(2,1)} %param.5), channel_id=1, source_target_pairs={{0,30},{2,0},{4,2},{6,4},{8,6},{10,8},{12,10},{14,12},{16,14},{18,... | collective-permute-start | bytes 5505032 | tf_op jit(solution)/shard_map/ppermute | solution.py:12
  34.5 16.9 %copy-start.3 = (bf16[32,224,256]{2,1,0:T(8,128)(2,1)}, bf16[32,224,256]{2,1,0:T(8,128)(2,1)S(1)}, u32[]{:S(2)}) copy-start(bf16[32,224,256]{2,1,0:T(8,128)(2,1)S(1)} %get-tuple-element.46) | copy-start | bytes 11010052
  34.7 16.6 %copy-start.1 = (bf16[32,224,256]{2,1,0:T(8,128)(2,1)}, bf16[32,224,256]{2,1,0:T(8,128)(2,1)S(1)}, u32[]{:S(2)}) copy-start(bf16[32,224,256]{2,1,0:T(8,128)(2,1)S(1)} %constant_dynamic-update-slice_fusion.2) | copy-start | bytes 11010052
  57.7 7.9 %copy-start.8 = (bf16[32,112,256]{2,1,0:T(8,128)(2,1)S(1)}, bf16[32,112,256]{2,1,0:T(8,128)(2,1)}, u32[]{:S(2)}) copy-start(bf16[32,112,256]{2,1,0:T(8,128)(2,1)} %param.6) | copy-start | bytes 5505028
  57.7 7.9 %copy-start.9 = (bf16[1024,256]{1,0:T(8,128)(2,1)S(1)}, bf16[1024,256]{1,0:T(8,128)(2,1)}, u32[]{:S(2)}) copy-start(bf16[1024,256]{1,0:T(8,128)(2,1)} %param.9) | copy-start | bytes 1572868
  65.6 42.0 %copy-start.7 = (bf16[3584,1024]{1,0:T(8,128)(2,1)}, bf16[3584,1024]{1,0:T(8,128)(2,1)S(1)}, u32[]{:S(2)}) copy-start(bf16[3584,1024]{1,0:T(8,128)(2,1)S(1)} %get-tuple-element.79) | copy-start | bytes 22020100
  80.9 3.1 copy-start.5
  89.5 5.4 %copy-start.2 = (bf16[32,224,256]{2,1,0:T(8,128)(2,1)S(1)}, bf16[32,224,256]{2,1,0:T(8,128)(2,1)}, u32[]{:S(2)}) copy-start(bf16[32,224,256]{2,1,0:T(8,128)(2,1)} %copy-done.1) | copy-start | bytes 11010052
  94.9 9.6 %copy-start.4 = (f32[3584,256]{1,0:T(8,128)}, f32[3584,256]{1,0:T(8,128)S(1)}, u32[]{:S(2)}) copy-start(f32[3584,256]{1,0:T(8,128)S(1)} %subtract_multiply_fusion) | copy-start | bytes 11010052
  113.3 118.0 %collective-permute-start.2 = (bf16[32,60,256]{2,0,1:T(8,128)(2,1)}, bf16[32,60,256]{2,0,1:T(8,128)(2,1)}, u32[]{:S(2)}, u32[]{:S(2)}) collective-permute-start(bf16[32,60,256]{2,0,1:T(8,128)(2,1)} %get-tuple-element.44), channel_id=1, source_target_pairs={{0,30},{2,0},{4,2},{6,4},{8,6},{10,8},{12,10},{14,12},{16,14},{18,... | collective-permute-start | bytes 2949128 | tf_op jit(solution)/shard_map/ppermute | solution.py:12
  117.2 112.2 %collective-permute-start.3 = (bf16[32,60,256]{2,0,1:T(8,128)(2,1)S(1)}, bf16[32,60,256]{2,0,1:T(8,128)(2,1)}, u32[]{:S(2)}, u32[]{:S(2)}) collective-permute-start(bf16[32,60,256]{2,0,1:T(8,128)(2,1)S(1)} %get-tuple-element.45), channel_id=1, source_target_pairs={{0,2},{2,4},{4,6},{6,8},{8,10},{10,12},{12,14},{14,16},{16,18},{18... | collective-permute-start | bytes 2949128 | tf_op jit(solution)/shard_map/ppermute | solution.py:12
  131.7 197.0 %all-reduce.5.cloned.1.call-start = ((), (), s32[]{:S(2)}) async-start(), calls=%async_computation | async-start | bytes 4194304 | tf_op jit(solution)/shard_map/psum | solution.py:106
Sparse Core Ops, SparseCore 0:
  131.8 64.6 all-reduce.6
  234.5 94.1 all-reduce.4
